TPU v7x, 32 devices: a whole 2x2x4 slice. The times are simulated.
32 devices in a mesh: parts: 2 (over y), col: 4 (over z), row: 4 (over x, core).
Axes of the slice: x: 2, y: 2, z: 4, core: 2. Of those that a mesh axis runs over, the one named last changes fastest.
Arguments:
- grad_table: bfloat16 [16384, 32768], P(('parts', 'row'), 'col'), parts along dimension 0, may hold values from -60 to 60
- prev_embed: bfloat16 [8192, 512], P('row', 'col'), may hold values from -6 to 6
- next_embed: bfloat16 [32768, 512], P('col', 'row'), may hold values from -6 to 6
- log_norm: float32 [16384], P(('parts', 'row')), parts along dimension 0, may hold values from 9 to 11
Outputs:
- prev_grad: float32 [16384, 512], P(('parts', 'row'), 'col'), parts along dimension 0
- next_grad: float32 [65536, 512], P(('parts', 'col'), 'row'), parts along dimension 0
There are 2 independent parts, one for each index of `parts`. A program takes and returns all parts, laid end to end along the dimension named above; an argument that names none is the same for every part. Nothing has to cross between parts.
All inputs are finite; a program needn't handle non-finite values.
Results may differ from a plain program's by a relative error of at most 0.0025.
Values may be sent and summed in bfloat16 or wider, within the bound.
No kernel may reach another device: no remote copies, remote signals or barrier semaphores. Data moves between devices by JAX's collectives and lax.ppermute only.
A program may use at most 256 MiB of HBM per device.

v0:
```python
import math

import jax
import jax.numpy as jnp
from jax import lax
from jax.sharding import PartitionSpec as P

E = 512


def body(grad_table, prev_embed, next_embed, log_norm):
    scale = 2.0 / math.sqrt(E)
    prev_full = lax.all_gather(prev_embed, "col", axis=1, tiled=True)
    next_full = lax.all_gather(next_embed, "row", axis=1, tiled=True)
    logits = lax.dot_general(
        prev_full, next_full, (((1,), (1,)), ((), ())), preferred_element_type=jnp.float32
    )
    probs = jnp.exp(scale * logits - log_norm[:, None])
    widened = grad_table.astype(jnp.float32)
    row_dot = lax.psum(jnp.sum(widened * probs, axis=1), "col")
    dlogits = (scale * probs * (widened - row_dot[:, None])).astype(jnp.bfloat16)
    next_terms = lax.dot_general(
        dlogits, prev_full, (((0,), (0,)), ((), ())), preferred_element_type=jnp.float32
    )
    next_grad = lax.psum_scatter(next_terms, "row", scatter_dimension=1, tiled=True)
    prev_terms = jnp.dot(dlogits, next_full, preferred_element_type=jnp.float32)
    prev_grad = lax.psum_scatter(prev_terms, "col", scatter_dimension=1, tiled=True)
    return (prev_grad, next_grad)


def solution(mesh):
    placed = (P(("parts", "row"), "col"), P("row", "col"), P("col", "row"), P(("parts", "row")))
    return jax.shard_map(
        body,
        mesh=mesh,
        in_specs=placed,
        out_specs=(P(("parts", "row"), "col"), P(("parts", "col"), "row")),
        check_vma=False,
    )
```

profile of v0, /device:TPU:0, one launch (start us, length us, event | category | flops | bytes accessed | tf_op | source)
XLA Modules:
  0.0 449.1 jit_solution(12746472674789742065)
XLA Ops:
  7.2 0.0 all-gather.3.cloned.1.call-start
  7.2 0.7 all-gather.3.cloned.1.call-update
  7.9 0.0 all-gather.5.cloned.1.call-start
  7.9 0.7 all-gather.5.cloned.1.call-update
  8.6 0.0 copy-start
  8.7 0.0 reduce-scatter.3.cloned.1.call-start
  8.7 49.8 %all-gather.3.cloned.1.call-done = bf16[2048,512]{1,0:T(8,128)(2,1)} async-done(((bf16[2048,128]{1,0:T(8,128)(2,1)}), bf16[2048,512]{1,0:T(8,128)(2,1)}) %all-gather.3.cloned.1.call-update) | async-done | bytes 2097168 | tf_op jit(solution)/shard_map/all_gather | solution.py:13
  58.5 59.1 %all-gather.5.cloned.1.call-done = bf16[8192,512]{1,0:T(8,128)(2,1)} async-done(((bf16[8192,128]{1,0:T(8,128)(2,1)}), bf16[8192,512]{1,0:T(8,128)(2,1)}) %all-gather.5.cloned.1.call-update) | async-done | bytes 8388624 | tf_op jit(solution)/shard_map/all_gather | solution.py:14
  117.7 42.7 %fusion = (f32[2048]{0:T(1024)S(1)}, f32[2048,8192]{1,0:T(8,128)}) fusion(bf16[2048,8192]{1,0:T(8,128)(2,1)} %param.4, f32[2048]{0:T(1024)} %param.7, bf16[2048,512]{1,0:T(8,128)(2,1)} %all-gather.3.cloned.1.call-done, bf16[8192,512]{1,0:T(8,128)(2,1)} %all-gather.5.cloned.1.call-done), kind=kOutput, calls=%fused_computation.2 | convolution fusion | flops 17263753216 | bytes 111165440 | tf_op jit(solution)/shard_map/dot_general | solution.py:15
  160.4 11.8 %psum.7 = f32[2048]{0:T(1024)S(1)} all-reduce(f32[2048]{0:T(1024)S(1)} %get-tuple-element.2), channel_id=1, replica_groups=mesh['parts'=2,'col'=4,'row'=4] {'col'}, use_global_device_ids=true, to_apply=%region_1.0 | all-reduce | flops 2048 | bytes 16384 | tf_op jit(solution)/shard_map/psum | solution.py:20
  172.3 0.0 copy-done
  172.3 42.8 %fusion.2 = bf16[2048,8192]{1,0:T(8,128)(2,1)} fusion(bf16[2048,8192]{1,0:T(8,128)(2,1)} %param.4, f32[2048,8192]{1,0:T(8,128)} %get-tuple-element.3, f32[2048]{0:T(1024)S(1)} %psum.7, f32[2048]{0:T(1024)S(1)} %copy-done), kind=kLoop, calls=%fused_computation.4 | loop fusion | flops 117440512 | bytes 134234112 | tf_op jit(solution)/shard_map/convert_element_type | solution.py:21
  215.1 0.0 copy-start.1
  215.1 24.9 %fusion.3 = f32[2048,512]{1,0:T(8,128)} fusion(bf16[2048,8192]{1,0:T(8,128)(2,1)} %fusion.2, bf16[8192,512]{1,0:T(8,128)(2,1)} %all-gather.5.cloned.1.call-done), kind=kOutput, calls=%fused_computation.6 | convolution fusion | flops 17179869184 | bytes 46137344 | tf_op jit(solution)/shard_map/dot_general | solution.py:26
  240.0 0.0 reduce-scatter.3.cloned.1.call-update
  240.0 0.2 reduce-scatter.5.cloned.1.call-start
  240.3 0.0 copy-done.1
  240.3 27.7 %fusion.4 = f32[8192,512]{1,0:T(8,128)} fusion(bf16[2048,8192]{1,0:T(8,128)(2,1)} %fusion.2, bf16[2048,512]{1,0:T(8,128)(2,1)S(1)} %copy-done.1), kind=kOutput, calls=%fused_computation.7 | convolution fusion | flops 17179869184 | bytes 52428800 | tf_op jit(solution)/shard_map/dot_general | solution.py:22
  268.0 0.0 reduce-scatter.5.cloned.1.call-update
  268.0 46.2 %reduce-scatter.3.cloned.1.call-done = f32[2048,128]{1,0:T(8,128)} async-done(((f32[2048,512]{1,0:T(8,128)}), f32[2048,128]{1,0:T(8,128)}) %reduce-scatter.3.cloned.1.call-update) | async-done | bytes 1048592 | tf_op jit(solution)/shard_map/reduce_scatter | solution.py:27
  314.2 128.4 %reduce-scatter.5.cloned.1.call-done = f32[8192,128]{1,0:T(8,128)} async-done(((f32[8192,512]{1,0:T(8,128)}), f32[8192,128]{1,0:T(8,128)}) %reduce-scatter.5.cloned.1.call-update) | async-done | bytes 4194320 | tf_op jit(solution)/shard_map/reduce_scatter | solution.py:25
Async XLA Ops:
  7.2 51.4 %all-gather.3.cloned.1.call-start = ((), (), s32[]{:S(2)}) async-start(), calls=%async_computation.2 | async-start | bytes 2621440 | tf_op jit(solution)/shard_map/all_gather | solution.py:13
  7.9 109.8 %all-gather.5.cloned.1.call-start = ((), (), s32[]{:S(2)}) async-start(), calls=%async_computation.3 | async-start | bytes 10485760 | tf_op jit(solution)/shard_map/all_gather | solution.py:14
  8.6 163.7 %copy-start = (f32[2048]{0:T(1024)S(1)}, f32[2048]{0:T(1024)}, u32[]{:S(2)}) copy-start(f32[2048]{0:T(1024)} %param.7) | copy-start | bytes 24580
  8.7 305.6 %reduce-scatter.3.cloned.1.call-start = ((), (), s32[]{:S(2)}) async-start(), calls=%async_computation.4 | async-start | bytes 5242880 | tf_op jit(solution)/shard_map/reduce_scatter | solution.py:27
  215.1 25.1 %copy-start.1 = (bf16[2048,512]{1,0:T(8,128)(2,1)S(1)}, bf16[2048,512]{1,0:T(8,128)(2,1)}, u32[]{:S(2)}) copy-start(bf16[2048,512]{1,0:T(8,128)(2,1)} %all-gather.3.cloned.1.call-done) | copy-start | bytes 6291460
  240.0 202.6 %reduce-scatter.5.cloned.1.call-start = ((), (), s32[]{:S(2)}) async-start(), calls=%async_computation.5 | async-start | bytes 20971520 | tf_op jit(solution)/shard_map/reduce_scatter | solution.py:25
Sparse Core Ops, SparseCore 0:
  9.5 48.9 all-gather.2
  60.1 57.5 all-gather.4
  240.2 74.0 reduce-scatter.2
  317.2 125.3 reduce-scatter.4
where the time goes:
time: 449 us
  waiting for transfers between devices  285 us (63%)
  matrix products  95.3 us (21%)
  other arithmetic  42.8 us (10%)
  between operations  13.8 us (3%)
  blocking collectives  11.8 us (3%)
    reduce_scatter x1, waiting for transfers between devices, body(): lax.psum_scatter(next_terms, 'row', scatter_dimension=1, tiled=True)  128 us
    all_gather x1, waiting for transfers between devices, body(): next_full = lax.all_gather(next_embed, 'row', axis=1, tiled=True)  59.1 us
    all_gather x1, waiting for transfers between devices, body(): prev_full = lax.all_gather(prev_embed, 'col', axis=1, tiled=True)  49.8 us
    reduce_scatter x1, waiting for transfers between devices, body(): lax.psum_scatter(prev_terms, 'col', scatter_dimension=1, tiled=True)  46.2 us
    convert_element_type x1, other arithmetic, body(): (scale * probs * (widened - row_dot[:, None])).astype(jnp.bfloat16)  42.8 us
    dot_general x1, matrix products, body(): lax.dot_general(prev_full, next_full, (((1,), (1,)), ((), ())), preferred...  42.7 us
    dot_general x1, matrix products, body(): lax.dot_general(dlogits, prev_full, (((0,), (0,)), ((), ())), preferred_e...  27.7 us
    dot_general x1, matrix products, body(): prev_terms = jnp.dot(dlogits, next_full, preferred_element_type=jnp.float32)  24.9 us
  transfers between devices with their start and end apart: 4, of which 4 were waited for; matrix products, arithmetic and copies ran while one was open for 6% of the time, Pallas kernels for 0%

commit v1 on v0

v1 whole, which is shorter than its diff:
```python
import functools
import math

import jax
import jax.numpy as jnp
from jax import lax
from jax.experimental import pallas as pl
from jax.experimental.pallas import tpu as pltpu
from jax.sharding import PartitionSpec as P


VMEM_LIMIT = 60 * 2**20
LOG2E = math.log2(math.e)


def xor_swap(x, axis, size, mask):
    return lax.ppermute(x, axis, [(i, i ^ mask) for i in range(size)])


def bits_of(size):
    if size & (size - 1):
        raise ValueError("axis size")
    return [1 << b for b in reversed(range(size.bit_length() - 1))]


def gather_pieces(own, axis, size):
    pieces = [(0, own)]
    for bit in bits_of(size):
        new = []
        for mask, piece in pieces:
            new.append((mask | bit, xor_swap(piece, axis, size, bit)))
        pieces += new
    return pieces


def slots_of(size):
    order = [0]
    for bit in bits_of(size):
        order = order + [mask | bit for mask in order]
    width = size.bit_length() - 1
    return sorted(order, key=lambda m: int(format(m, f"0{width}b")[::-1], 2) if width else 0)


def slot(mask, size):
    width = size.bit_length() - 1
    out = 0
    for b in range(width):
        out = out + ((mask >> b) & 1) * (1 << (width - 1 - b))
    return out


def pass1_kernel(masks_p, masks_n, first, with_t, sub, *refs):
    scal, refs = refs[0], list(refs[1:])
    prev = [refs.pop(0) for _ in masks_p]
    nxt = [refs.pop(0) for _ in masks_n]
    grad, norm = refs.pop(0), refs.pop(0)
    dot_in = None if first[1] else refs.pop(0)
    if not first[0]:
        refs.pop(0)
    table, dot_out = refs.pop(0), refs.pop(0)
    turned = refs.pop(0) if with_t else None
    left, right, acc, norms = refs
    rows, width = table.shape
    step = pl.program_id(0)

    @pl.when(step == 0)
    def _():
        for mask, ref in zip(masks_p, prev):
            w = ref.shape[1]
            at = pl.multiple_of((scal[0] ^ mask) * w, w) if len(masks_p) > 1 else 0
            left[:, pl.ds(at, w)] = ref[...]
        acc[...] = jnp.zeros_like(acc)
        norms[...] = jnp.transpose(jnp.broadcast_to(norm[...] * LOG2E, (128, rows)))
        if with_t:
            turned[...] = jnp.transpose(left[...])

    for mask, ref in zip(masks_n, nxt):
        w = ref.shape[1]
        at = pl.multiple_of((scal[1] ^ mask) * w, w) if len(masks_n) > 1 else 0
        right[:, pl.ds(at, w)] = ref[...]
    scale = 2.0 / math.sqrt(left.shape[1]) * LOG2E
    x = left[...]
    total = acc[...]
    base = norms[...]
    for j in range(width // sub):
        s = slice(j * sub, (j + 1) * sub)
        logits = lax.dot_general(
            x, right[s, :], (((1,), (1,)), ((), ())), preferred_element_type=jnp.float32
        )
        probs = jnp.exp2(scale * logits - jnp.concatenate([base] * (sub // 128), axis=1))
        table[:, s] = probs
        terms = grad[:, s].astype(jnp.float32) * probs
        for t in range(sub // 128):
            total = total + terms[:, t * 128 : (t + 1) * 128]
    acc[...] = total

    @pl.when(step == pl.num_programs(0) - 1)
    def _():
        sums = jnp.sum(jnp.transpose(total), axis=0, keepdims=True)
        dot_out[...] = sums if dot_in is None else sums + dot_in[...]


def pass1(scal, prev, nxt, grad, norm, dot_in, table, start, with_t):
    rows = prev[0][1].shape[0]
    cols = nxt[0][1].shape[0]
    features = sum(p.shape[1] for _, p in prev)
    tile = min(1024, cols)
    off = start // tile
    args = [p for _, p in prev] + [p for _, p in nxt] + [grad, norm]
    specs = [pl.BlockSpec((rows, p.shape[1]), lambda c, s: (0, 0)) for _, p in prev]
    specs += [pl.BlockSpec((tile, p.shape[1]), lambda c, s: (c, 0)) for _, p in nxt]
    specs += [
        pl.BlockSpec((rows, tile), lambda c, s: (0, c + off)),
        pl.BlockSpec((1, rows), lambda c, s: (0, 0)),
    ]
    if dot_in is not None:
        args.append(dot_in)
        specs.append(pl.BlockSpec((1, rows), lambda c, s: (0, 0)))
    alias = {}
    if table is not None:
        alias = {1 + len(args): 0}
        args.append(table)
        specs.append(pl.BlockSpec(memory_space=pl.ANY))
    shapes = [
        jax.ShapeDtypeStruct(grad.shape, jnp.float32),
        jax.ShapeDtypeStruct((1, rows), jnp.float32),
    ]
    outs = [
        pl.BlockSpec((rows, tile), lambda c, s: (0, c + off)),
        pl.BlockSpec((1, rows), lambda c, s: (0, 0)),
    ]
    if with_t:
        shapes.append(jax.ShapeDtypeStruct((features, rows), jnp.bfloat16))
        outs.append(pl.BlockSpec((features, rows), lambda c, s: (0, 0)))
    return pl.pallas_call(
        functools.partial(
            pass1_kernel,
            [m for m, _ in prev],
            [m for m, _ in nxt],
            (table is None, dot_in is None),
            with_t,
            256,
        ),
        grid_spec=pltpu.PrefetchScalarGridSpec(
            num_scalar_prefetch=1,
            grid=(cols // tile,),
            in_specs=specs,
            out_specs=outs,
            scratch_shapes=[
                pltpu.VMEM((rows, features), jnp.bfloat16),
                pltpu.VMEM((tile, features), jnp.bfloat16),
                pltpu.VMEM((rows, 128), jnp.float32),
                pltpu.VMEM((rows, 128), jnp.float32),
            ],
        ),
        out_shape=shapes,
        input_output_aliases=alias,
        cost_estimate=pl.CostEstimate(
            flops=2 * rows * cols * features,
            bytes_accessed=rows * cols * 6,
            transcendentals=rows * cols,
        ),
        compiler_params=pltpu.CompilerParams(
            dimension_semantics=("arbitrary",), vmem_limit_bytes=VMEM_LIMIT
        ),
    )(scal, *args)


def pass2_kernel(masks_n, n_col, n_row, n_dots, modes, sub, *refs):
    add_next, end_next, add_prev, end_prev = modes
    scal, refs = refs[0], list(refs[1:])
    turned = [refs.pop(0) for _ in range(n_row)]
    nxt = [refs.pop(0) for _ in masks_n]
    grad, table = refs.pop(0), refs.pop(0)
    dots = [refs.pop(0) for _ in range(n_dots)]
    refs.pop(0)
    next_in = refs.pop(0) if add_next else None
    prev_in = refs.pop(0) if add_prev else None
    token = refs.pop(0)
    next_out = [refs.pop(0) for _ in range(1 + end_next)]
    prev_out = [refs.pop(0) for _ in range(1 + end_prev)]
    right, dot_cols = refs[0], refs[1]
    acc = refs[2] if end_prev else prev_out[0]
    rows, width = table.shape
    step = pl.program_id(0)
    features = right.shape[1]
    half = features // 2

    @pl.when(step == 0)
    def _():
        row = dots[0][...]
        for ref in dots[1:]:
            row = row + ref[...]
        dot_cols[...] = jnp.transpose(jnp.broadcast_to(row, (128, rows)))
        acc[...] = prev_in[...] if add_prev else jnp.zeros_like(acc)
        token[...] = jnp.zeros_like(token)

    for mask, ref in zip(masks_n, nxt):
        w = ref.shape[1]
        at = 0
        if len(masks_n) > 1:
            at = pl.multiple_of(slot((scal[1] ^ mask) ^ scal[0], n_col) * w, w)
        right[:, pl.ds(at, w)] = ref[...]
    scale = 2.0 / math.sqrt(features)
    left = jnp.concatenate([ref[...] for ref in turned], axis=0)
    base = dot_cols[...]
    total = None
    for j in range(width // sub):
        s = slice(j * sub, (j + 1) * sub)
        wide = grad[:, s].astype(jnp.float32)
        shift = jnp.concatenate([base] * (sub // 128), axis=1)
        d = ((scale * table[:, s]) * (wide - shift)).astype(jnp.bfloat16)
        t = jnp.dot(left, d, preferred_element_type=jnp.float32)
        if add_next:
            t = t + next_in[:, s]
        if end_next:
            next_out[0][:, s] = t[:half]
            next_out[1][:, s] = t[half:].astype(jnp.bfloat16)
        else:
            next_out[0][:, s] = t
        q = jnp.dot(d, right[s, :], preferred_element_type=jnp.float32)
        total = q if total is None else total + q
    acc[...] += total

    if end_prev:

        @pl.when(step == pl.num_programs(0) - 1)
        def _():
            prev_out[0][...] = acc[:, :half]
            prev_out[1][...] = acc[:, half:].astype(jnp.bfloat16)


def pass2(scal, turned, nxt, grad, table, dots, token, next_in, prev_in, row0, rows, start, cols,
          piece_start, n_col, n_row, end_next, end_prev):
    features = turned.shape[0]
    tile = min(1024, cols)
    off, poff, rb = start // tile, (start - piece_start) // tile, row0 // rows
    order = slots_of(n_row)
    w = features // n_row
    once = pl.Buffered(1)
    args = [turned] * n_row + [p for _, p in nxt] + [grad, table, *dots, token]
    specs = [
        pl.BlockSpec((w, rows), lambda c, s, m=m: (s[1] ^ m, rb), pipeline_mode=once)
        for m in order
    ]
    specs += [pl.BlockSpec((tile, p.shape[1]), lambda c, s: (c + poff, 0)) for _, p in nxt]
    specs += [pl.BlockSpec((rows, tile), lambda c, s: (rb, c + off))] * 2
    specs += [pl.BlockSpec((1, rows), lambda c, s: (0, rb)) for _ in dots]
    specs += [pl.BlockSpec(memory_space=pl.ANY)]
    if next_in is not None:
        args.append(next_in)
        specs.append(pl.BlockSpec((features, tile), lambda c, s: (0, c)))
    if prev_in is not None:
        pb = 0 if prev_in.shape[0] == rows else rb
        args.append(prev_in)
        specs.append(pl.BlockSpec((rows, features), lambda c, s: (pb, 0), pipeline_mode=once))
    half = features // 2
    f32, bf16 = jnp.float32, jnp.bfloat16
    shapes = [jax.ShapeDtypeStruct((8, 128), f32)]
    outs = [pl.BlockSpec((8, 128), lambda c, s: (0, 0))]
    kinds = [(half, f32), (half, bf16)] if end_next else [(features, f32)]
    for h, kind in kinds:
        shapes.append(jax.ShapeDtypeStruct((h, cols), kind))
        outs.append(pl.BlockSpec((h, tile), lambda c, s: (0, c)))
    kinds = [(half, f32), (half, bf16)] if end_prev else [(features, f32)]
    for h, kind in kinds:
        shapes.append(jax.ShapeDtypeStruct((rows, h), kind))
        outs.append(pl.BlockSpec((rows, h), lambda c, s: (0, 0)))
    scratch = [pltpu.VMEM((tile, features), bf16), pltpu.VMEM((rows, 128), f32)]
    if end_prev:
        scratch.append(pltpu.VMEM((rows, features), f32))
    out = pl.pallas_call(
        functools.partial(
            pass2_kernel,
            [m for m, _ in nxt],
            n_col,
            n_row,
            len(dots),
            (next_in is not None, end_next, prev_in is not None, end_prev),
            min(512, tile),
        ),
        grid_spec=pltpu.PrefetchScalarGridSpec(
            num_scalar_prefetch=1,
            grid=(cols // tile,),
            in_specs=specs,
            out_specs=outs,
            scratch_shapes=scratch,
        ),
        out_shape=shapes,
        cost_estimate=pl.CostEstimate(
            flops=4 * rows * cols * features, bytes_accessed=rows * cols * 6, transcendentals=0
        ),
        compiler_params=pltpu.CompilerParams(
            dimension_semantics=("arbitrary",), vmem_limit_bytes=VMEM_LIMIT
        ),
    )(scal, *args)
    split = 2 + end_next
    return out[0], tuple(out[1:split]), tuple(out[split:])


def turn_kernel(keep, got, *refs):
    refs[-1][...] = jnp.transpose(keep[...] + got[...].astype(jnp.float32))


def turn_into(out, keep, got, start, cols):
    w, width = keep.shape
    tile = min(1024, width)
    off = start // tile
    args = [keep, got]
    specs = [pl.BlockSpec((w, tile), lambda c: (0, c))] * 2
    alias = {}
    if out is not None:
        args.append(out)
        specs.append(pl.BlockSpec(memory_space=pl.ANY))
        alias = {2: 0}
    return pl.pallas_call(
        turn_kernel,
        grid=(width // tile,),
        in_specs=specs,
        out_specs=pl.BlockSpec((tile, w), lambda c: (c + off, 0)),
        out_shape=jax.ShapeDtypeStruct((cols, w), jnp.float32),
        input_output_aliases=alias,
        cost_estimate=pl.CostEstimate(
            flops=w * width, bytes_accessed=w * width * 10, transcendentals=0
        ),
        compiler_params=pltpu.CompilerParams(dimension_semantics=("arbitrary",)),
    )(*args)


def halve_sums(keep, send, axis, size, dim):
    for bit in reversed(bits_of(size)):
        got = xor_swap(send, axis, size, bit)
        if bit * 2 == size:
            return keep, got
        keep = keep + got.astype(jnp.float32)
        count = keep.shape[dim]
        send = lax.slice_in_dim(keep, count // 2, count, axis=dim).astype(jnp.bfloat16)
        keep = lax.slice_in_dim(keep, 0, count // 2, axis=dim)


def assembled(pieces, index):
    where = sorted(range(len(pieces)), key=lambda i: pieces[i][0])
    stack = jnp.stack([pieces[i][1] for i in where], axis=1)
    out = jnp.take(stack, jnp.arange(len(pieces)) ^ index, axis=1)
    return out.reshape(out.shape[0], -1)


def make_body(n_col, n_row):
    def body(grad, prev_own, next_own, log_norm):
        rows, cols = grad.shape
        z, r = lax.axis_index("col"), lax.axis_index("row")
        scal = jnp.stack([z, r]).astype(jnp.int32)
        norm = log_norm[None, :]
        half, quarter = cols // 2, cols // 4
        placed = prev_own.shape[1] % 128 == 0 and prev_own.shape[1] == next_own.shape[1]

        prev = gather_pieces(prev_own, "col", n_col)
        if not placed:
            prev = [(0, assembled(prev, z))]

        def next_chunk(c):
            own = lax.slice_in_dim(next_own, c * half, (c + 1) * half)
            pieces = gather_pieces(own, "row", n_row)
            if placed:
                return pieces, pieces
            full = assembled(pieces, r)
            blocks = full.reshape(half, n_col, -1)
            order = jnp.array(slots_of(n_col)) ^ z
            return [(0, full)], [(0, jnp.take(blocks, order, axis=1).reshape(full.shape))]

        chunks = [next_chunk(c) for c in range(2)]
        table, dot, turned = pass1(
            scal, prev, chunks[0][0], grad, norm, None, None, 0, True
        )
        table, dot = pass1(scal, prev, chunks[1][0], grad, norm, dot, table, half, False)
        if n_col <= 4:
            dots = [dot] + [xor_swap(dot, "col", n_col, m) for m in range(1, n_col)]
        else:
            dots = [lax.psum(dot, "col")]

        token = jnp.zeros((8, 128), jnp.float32)
        mid = rows // 2
        last = half + quarter
        plan = [
            (0, rows, 0, half),
            (0, rows, half, quarter),
            (0, mid, last, quarter),
            (mid, mid, last, quarter),
        ]
        prev_sum, next_part, next_done, prev_done = None, None, {}, []
        for row0, height, start, width in plan:
            c = start // half
            end_prev, end_next = height < rows, row0 + height == rows
            token, n_out, p_out = pass2(
                scal, turned, chunks[c][1], grad, table, dots, token, next_part, prev_sum,
                row0, height, start, width, c * half, n_col, n_row, end_next, end_prev,
            )
            if end_next:
                next_done[start] = halve_sums(*n_out, "row", n_row, 0)
            else:
                next_part = n_out[0]
            if end_prev:
                prev_done.append(halve_sums(*p_out, "col", n_col, 1))
            else:
                prev_sum = p_out[0]
        next_grad = None
        for start in sorted(next_done):
            next_grad = turn_into(next_grad, *next_done[start], start, cols)
        prev_grad = jnp.concatenate([k + g.astype(jnp.float32) for k, g in prev_done], axis=0)
        return (prev_grad, next_grad)

    return body


def solution(mesh):
    placed = (P(("parts", "row"), "col"), P("row", "col"), P("col", "row"), P(("parts", "row")))
    n_col, n_row = mesh.shape["col"], mesh.shape["row"]
    return jax.shard_map(
        make_body(n_col, n_row),
        mesh=mesh,
        in_specs=placed,
        out_specs=(P(("parts", "row"), "col"), P(("parts", "col"), "row")),
        check_vma=False,
    )
```

time: 449 us -> 279 us (0.62)
  waiting for transfers between devices: 285 us -> 108 us
  Pallas kernels: 0 us -> 134 us
  matrix products: 95.3 us -> 0 us
  other arithmetic: 42.8 us -> 4.7 us
  starting transfers between devices: 0.34 us -> 19.8 us
  between operations: 13.8 us -> 0.9 us
  local copies, waits for them, and re-layouts: 0.01 us -> 11.9 us
  blocking collectives: 11.8 us -> 0 us
    reduce_scatter x2 -> x0, waiting for transfers between devices: 175 us -> none  [the longest x1 128 us: body(): lax.psum_scatter(next_terms, 'row', scatter_dimension=1, tiled=True)]
    pallas_call x0 -> x9, Pallas kernels: none -> 134 us  [the longest x4 74 us: pass2(): pl.pallas_call(functools.partial(pass2_kernel, [m for m, _ in nxt], n_col...]
    all_gather x2 -> x0, waiting for transfers between devices: 109 us -> none  [the longest x1 59.1 us: body(): next_full = lax.all_gather(next_embed, 'row', axis=1, tiled=True)]
    ppermute x0 -> x22, waiting for transfers between devices: none -> 108 us  [xor_swap(): return lax.ppermute(x, axis, [(i, i ^ mask) for i in range(size)])]
    dot_general x3 -> x0, matrix products: 95.3 us -> none  [the longest x1 42.7 us: body(): lax.dot_general(prev_full, next_full, (((1,), (1,)), ((), ())), preferred...]
    convert_element_type x1 -> x0, other arithmetic: 42.8 us -> none  [body(): (scale * probs * (widened - row_dot[:, None])).astype(jnp.bfloat16)]
    ppermute x0 -> x22, starting transfers between devices: none -> 19.8 us  [xor_swap(): return lax.ppermute(x, axis, [(i, i ^ mask) for i in range(size)])]
    psum x1 -> x0, blocking collectives: 11.8 us -> none  [body(): row_dot = lax.psum(jnp.sum(widened * probs, axis=1), 'col')]
  transfers between devices with their start and end apart: 4 -> 22, of which waited for: 4 -> 11; matrix products, arithmetic and copies ran while one was open for 6% -> 3% of each run, Pallas kernels for 0% -> 28%
where the time goes in v1:
time: 279 us
  Pallas kernels  134 us (48%)
  waiting for transfers between devices  108 us (39%)
  starting transfers between devices  19.8 us (7%)
  local copies, waits for them, and re-layouts  11.9 us (4%)
  other arithmetic  4.7 us (2%)
    ppermute x22, waiting for transfers between devices, xor_swap(): return lax.ppermute(x, axis, [(i, i ^ mask) for i in range(size)])  108 us
    pallas_call x4, Pallas kernels, pass2(): pl.pallas_call(functools.partial(pass2_kernel, [m for m, _ in nxt], n_col...  74 us
    pallas_call x2, Pallas kernels, pass1(): pl.pallas_call(functools.partial(pass1_kernel, [m for m, _ in prev], [m f...  50.8 us
    ppermute x22, starting transfers between devices, xor_swap(): return lax.ppermute(x, axis, [(i, i ^ mask) for i in range(size)])  19.8 us
    pallas_call x3, Pallas kernels, turn_into(): pl.pallas_call(turn_kernel, grid=(width // tile,), in_specs=specs, out_sp...  8.95 us
  transfers between devices with their start and end apart: 22, of which 11 were waited for; matrix products, arithmetic and copies ran while one was open for 3% of the time, Pallas kernels for 28%

profile of v1, /device:TPU:0, one launch (start us, length us, event | category | flops | bytes accessed | tf_op | source)
XLA Modules:
  0.0 278.9 jit_solution(3027866963797141059)
XLA Ops:
  0.6 0.0 copy-start.4
  0.6 2.7 fusion
  3.3 3.0 %collective-permute-start.3 = (bf16[4096,128]{1,0:T(8,128)(2,1)}, bf16[4096,128]{1,0:T(8,128)(2,1)}, u32[]{:S(2)}, u32[]{:S(2)}) collective-permute-start(bf16[4096,128]{1,0:T(8,128)(2,1)} %get-tuple-element.45.refs_5_), channel_id=1, source_target_pairs={{0,2},{1,3},{2,0},{3,1},{4,6},{5,7},{6,4},{7,5},{8,10},{9,11},{10,... | collective-permute-start | bytes 3145736 | tf_op jit(solution)/shard_map/ppermute | solution.py:17
  6.3 0.0 collective-permute-start.6
  6.3 3.1 %collective-permute-start = (bf16[2048,128]{1,0:T(8,128)(2,1)S(1)}, bf16[2048,128]{1,0:T(8,128)(2,1)}, u32[]{:S(2)}, u32[]{:S(2)}) collective-permute-start(bf16[2048,128]{1,0:T(8,128)(2,1)S(1)} %copy-done.4), channel_id=1, source_target_pairs={{0,8},{4,12},{8,0},{12,4},{1,9},{5,13},{9,1},{13,5},{2,10},{6,14},... | collective-permute-start | bytes 1572872 | tf_op jit(solution)/shard_map/ppermute | solution.py:17
  9.4 21.2 %collective-permute-done.3.refs_6_ = bf16[4096,128]{1,0:T(8,128)(2,1)} collective-permute-done((bf16[4096,128]{1,0:T(8,128)(2,1)}, bf16[4096,128]{1,0:T(8,128)(2,1)}, u32[]{:S(2)}, u32[]{:S(2)}) %collective-permute-start.3) | collective-permute-done | bytes 1048608 | tf_op jit(solution)/shard_map/ppermute | solution.py:17
  30.6 0.0 collective-permute-start.5
  30.6 2.1 collective-permute-start.1
  32.8 0.1 collective-permute-start.2
  32.8 12.7 %collective-permute-done.1.refs_3_ = bf16[2048,128]{1,0:T(8,128)(2,1)S(1)} collective-permute-done((bf16[2048,128]{1,0:T(8,128)(2,1)S(1)}, bf16[2048,128]{1,0:T(8,128)(2,1)S(1)}, u32[]{:S(2)}, u32[]{:S(2)}) %collective-permute-start.1) | collective-permute-done | bytes 524320 | tf_op jit(solution)/shard_map/ppermute | solution.py:17
  45.5 0.0 collective-permute-start.7
  45.5 6.6 %collective-permute-done.6.refs_6_ = bf16[4096,128]{1,0:T(8,128)(2,1)S(1)} collective-permute-done((bf16[4096,128]{1,0:T(8,128)(2,1)S(1)}, bf16[4096,128]{1,0:T(8,128)(2,1)S(1)}, u32[]{:S(2)}, u32[]{:S(2)}) %collective-permute-start.6) | collective-permute-done | bytes 1048608 | tf_op jit(solution)/shard_map/ppermute | solution.py:17
  52.2 0.0 collective-permute-start.8
  52.2 0.7 pad_add_fusion.refs_0_
  52.9 3.8 %collective-permute-done.2.refs_4_ = bf16[2048,128]{1,0:T(8,128)(2,1)} collective-permute-done((bf16[2048,128]{1,0:T(8,128)(2,1)}, bf16[2048,128]{1,0:T(8,128)(2,1)}, u32[]{:S(2)}, u32[]{:S(2)}) %collective-permute-start.2) | collective-permute-done | bytes 524320 | tf_op jit(solution)/shard_map/ppermute | solution.py:17
  56.7 25.9 %shard_map.59 = (f32[2048,8192]{1,0:T(8,128)}, f32[1,2048]{1,0:T(1,128)}, bf16[512,2048]{1,0:T(8,128)(2,1)}) custom-call(s32[2]{0:T(128)} %pad_add_fusion.refs_0_, bf16[2048,128]{1,0:T(8,128)(2,1)} %refs_1_.3, bf16[2048,128]{1,0:T(8,128)(2,1)} %collective-permute-done.refs_2_, bf16[2048,128]{1,0:T(8,128)(2,1)} %copy-done.5, ...), custom_call_target="tpu_custom_call" | custom-call | flops 8589934592 | bytes 50331648 | tf_op jit(solution)/shard_map/pallas_call | solution.py:135
  82.6 0.0 collective-permute-done.7.refs_7_
  82.7 0.0 collective-permute-done.8.refs_8_
  82.7 1.0 copy-done.2
  83.6 24.9 %shard_map.60 = (f32[2048,8192]{1,0:T(8,128)}, f32[1,2048]{1,0:T(1,128)}) custom-call(s32[2]{0:T(128)} %pad_add_fusion.refs_0_, bf16[2048,128]{1,0:T(8,128)(2,1)} %refs_1_.3, bf16[2048,128]{1,0:T(8,128)(2,1)} %collective-permute-done.refs_2_, bf16[2048,128]{1,0:T(8,128)(2,1)} %copy-done.5, ...), custom_call_target="tpu_custom_call", output_to_operand_aliasing={{0}: (12, {})} | custom-call | flops 8589934592 | bytes 50331648 | tf_op jit(solution)/shard_map/pallas_call | solution.py:135
  108.5 1.8 collective-permute-start.9
  110.3 2.6 collective-permute-start.10
  112.9 0.1 collective-permute-start.11
  112.9 2.1 collective-permute-done.10.refs_13_
  115.0 3.5 %collective-permute-done.11.refs_14_ = f32[1,2048]{1,0:T(1,128)S(1)} collective-permute-done((f32[1,2048]{1,0:T(1,128)}, f32[1,2048]{1,0:T(1,128)S(1)}, u32[]{:S(2)}, u32[]{:S(2)}) %collective-permute-start.11) | collective-permute-done | bytes 8224 | tf_op jit(solution)/shard_map/ppermute | solution.py:17
  118.5 0.6 broadcast_in_dim.7.refs_15_
  119.1 28.1 %shard_map.61 = (f32[8,128]{1,0:T(8,128)}, f32[256,4096]{1,0:T(8,128)}, bf16[256,4096]{1,0:T(8,128)(2,1)}, f32[2048,512]{1,0:T(8,128)}) custom-call(s32[2]{0:T(128)} %pad_add_fusion.refs_0_, bf16[512,2048]{1,0:T(8,128)(2,1)} %get-tuple-element.23.refs_1_.refs_2_.refs_3_.refs_4_, bf16[512,2048]{1,0:T(8,128)(2,1)} %get-tuple-element.23.refs_1_.refs_2_.refs_3_.refs_4_, ...), custom_call_target="tpu_custom_call" | custom-call | flops 17179869184 | bytes 50331648 | tf_op jit(solution)/shard_map/pallas_call | solution.py:272
  147.3 0.1 collective-permute-start.20
  147.4 19.5 %shard_map.62 = (f32[8,128]{1,0:T(8,128)}, f32[256,2048]{1,0:T(8,128)}, bf16[256,2048]{1,0:T(8,128)(2,1)}, f32[2048,512]{1,0:T(8,128)}) custom-call(s32[2]{0:T(128)} %pad_add_fusion.refs_0_, bf16[512,2048]{1,0:T(8,128)(2,1)} %get-tuple-element.23.refs_1_.refs_2_.refs_3_.refs_4_, bf16[512,2048]{1,0:T(8,128)(2,1)} %get-tuple-element.23.refs_1_.refs_2_.refs_3_.refs_4_, ...), custom_call_target="tpu_custom_call" | custom-call | flops 8589934592 | bytes 25165824 | tf_op jit(solution)/shard_map/pallas_call | solution.py:272
  166.9 12.3 %shard_map.63 = (f32[8,128]{1,0:T(8,128)}, f32[512,2048]{1,0:T(8,128)}, f32[1024,256]{1,0:T(8,128)}, bf16[1024,256]{1,0:T(8,128)(2,1)}) custom-call(s32[2]{0:T(128)} %pad_add_fusion.refs_0_, bf16[512,2048]{1,0:T(8,128)(2,1)} %get-tuple-element.23.refs_1_.refs_2_.refs_3_.refs_4_, bf16[512,2048]{1,0:T(8,128)(2,1)} %get-tuple-element.23.refs_1_.refs_2_.refs_3_.refs_4_, ...), custom_call_target="tpu_custom_call" | custom-call | flops 4294967296 | bytes 12582912 | tf_op jit(solution)/shard_map/pallas_call | solution.py:272
  179.2 14.0 %shard_map.64 = (f32[8,128]{1,0:T(8,128)}, f32[256,2048]{1,0:T(8,128)}, bf16[256,2048]{1,0:T(8,128)(2,1)}, f32[1024,256]{1,0:T(8,128)}, bf16[1024,256]{1,0:T(8,128)(2,1)}) custom-call(s32[2]{0:T(128)} %pad_add_fusion.refs_0_, bf16[512,2048]{1,0:T(8,128)(2,1)} %get-tuple-element.23.refs_1_.refs_2_.refs_3_.refs_4_, ...), custom_call_target="tpu_custom_call" | custom-call | flops 4294967296 | bytes 12582912 | tf_op jit(solution)/shard_map/pallas_call | solution.py:272
  193.2 0.1 collective-permute-start.14
  193.3 0.6 collective-permute-start.16
  193.9 1.7 collective-permute-start.12
  195.6 12.7 %collective-permute-done.14 = bf16[1024,256]{1,0:T(8,128)(2,1)S(1)} collective-permute-done((bf16[1024,256]{1,0:T(8,128)(2,1)}, bf16[1024,256]{1,0:T(8,128)(2,1)S(1)}, u32[]{:S(2)}, u32[]{:S(2)}) %collective-permute-start.14) | collective-permute-done | bytes 524320 | tf_op jit(solution)/shard_map/ppermute | solution.py:17
  208.3 1.3 convert_add_fusion.3
  209.7 0.1 collective-permute-start.15
  209.8 15.0 %collective-permute-done.12 = bf16[1024,256]{1,0:T(8,128)(2,1)S(1)} collective-permute-done((bf16[1024,256]{1,0:T(8,128)(2,1)S(1)}, bf16[1024,256]{1,0:T(8,128)(2,1)S(1)}, u32[]{:S(2)}, u32[]{:S(2)}) %collective-permute-start.12) | collective-permute-done | bytes 524320 | tf_op jit(solution)/shard_map/ppermute | solution.py:17
  224.7 0.1 convert_add_fusion.4
  224.9 0.1 collective-permute-start.13
  225.0 0.0 copy-start.3
  225.0 0.3 convert_add_fusion.2
  225.3 0.1 slice.72
  225.4 1.6 collective-permute-start.17
  226.9 0.2 copy-done.3
  227.2 0.8 convert_add_fusion
  227.9 0.1 slice.70
  228.1 1.6 collective-permute-start.21
  229.6 0.4 convert_add_fusion.1
  230.0 0.9 slice.71
  230.9 1.4 collective-permute-start.19
  232.3 5.8 %collective-permute-done.13 = bf16[1024,128]{1,0:T(8,128)(2,1)S(1)} collective-permute-done((bf16[1024,128]{1,0:T(8,128)(2,1)S(1)}, bf16[1024,128]{1,0:T(8,128)(2,1)S(1)}, u32[]{:S(2)}, u32[]{:S(2)}) %collective-permute-start.13) | collective-permute-done | bytes 262176 | tf_op jit(solution)/shard_map/ppermute | solution.py:17
  238.2 1.0 pad_maximum_fusion
  239.3 1.1 slice.57.keep
  240.3 1.1 slice.59.keep
  241.4 1.5 slice.61.keep
  242.9 19.8 %collective-permute-done.21.got = bf16[128,4096]{1,0:T(8,128)(2,1)S(1)} collective-permute-done((bf16[128,4096]{1,0:T(8,128)(2,1)S(1)}, bf16[128,4096]{1,0:T(8,128)(2,1)S(1)}, u32[]{:S(2)}, u32[]{:S(2)}) %collective-permute-start.21) | collective-permute-done | bytes 1048608 | tf_op jit(solution)/shard_map/ppermute | solution.py:17
  262.7 1.0 copy-done.8
  263.7 4.3 %shard_map.65.refs_0_ = f32[8192,128]{1,0:T(8,128)} custom-call(f32[128,4096]{1,0:T(8,128)} %slice.61.keep, bf16[128,4096]{1,0:T(8,128)(2,1)} %copy-done.8), custom_call_target="tpu_custom_call" | custom-call | flops 524288 | bytes 5242880 | tf_op jit(solution)/shard_map/pallas_call | solution.py:316
  268.0 4.7 %collective-permute-done.19.got = bf16[128,2048]{1,0:T(8,128)(2,1)S(1)} collective-permute-done((bf16[128,2048]{1,0:T(8,128)(2,1)}, bf16[128,2048]{1,0:T(8,128)(2,1)S(1)}, u32[]{:S(2)}, u32[]{:S(2)}) %collective-permute-start.19) | collective-permute-done | bytes 524320 | tf_op jit(solution)/shard_map/ppermute | solution.py:17
  272.6 0.8 copy-done.11
  273.4 2.3 shard_map.66.refs_0_
  275.8 0.8 copy-done.10
  276.6 2.3 shard_map.67
  (40 shorter events, 0.2 us)
Async XLA Ops:
  0.6 5.7 %copy-start.4 = (bf16[2048,128]{1,0:T(8,128)(2,1)S(1)}, bf16[2048,128]{1,0:T(8,128)(2,1)}, u32[]{:S(2)}) copy-start(bf16[2048,128]{1,0:T(8,128)(2,1)} %refs_1_.3) | copy-start | bytes 1572868
  3.3 79.3 %copy-start = (bf16[4096,128]{1,0:T(8,128)(2,1)}, bf16[4096,128]{1,0:T(8,128)(2,1)S(1)}, u32[]{:S(2)}) copy-start(bf16[4096,128]{1,0:T(8,128)(2,1)S(1)} %get-tuple-element.44.refs_5_) | copy-start | bytes 3145732
  3.3 27.3 %collective-permute-start.3 = (bf16[4096,128]{1,0:T(8,128)(2,1)}, bf16[4096,128]{1,0:T(8,128)(2,1)}, u32[]{:S(2)}, u32[]{:S(2)}) collective-permute-start(bf16[4096,128]{1,0:T(8,128)(2,1)} %get-tuple-element.45.refs_5_), channel_id=1, source_target_pairs={{0,2},{1,3},{2,0},{3,1},{4,6},{5,7},{6,4},{7,5},{8,10},{9,11},{10,... | collective-permute-start | bytes 3145736 | tf_op jit(solution)/shard_map/ppermute | solution.py:17
  6.3 45.8 %collective-permute-start.6 = (bf16[4096,128]{1,0:T(8,128)(2,1)S(1)}, bf16[4096,128]{1,0:T(8,128)(2,1)S(1)}, u32[]{:S(2)}, u32[]{:S(2)}) collective-permute-start(bf16[4096,128]{1,0:T(8,128)(2,1)S(1)} %get-tuple-element.44.refs_5_), channel_id=1, source_target_pairs={{0,2},{1,3},{2,0},{3,1},{4,6},{5,7},{6,4},{7,5},{8,10},{9,11},{10,... | collective-permute-start | bytes 3145736 | tf_op jit(solution)/shard_map/ppermute | solution.py:17
  6.3 26.4 %collective-permute-start = (bf16[2048,128]{1,0:T(8,128)(2,1)S(1)}, bf16[2048,128]{1,0:T(8,128)(2,1)}, u32[]{:S(2)}, u32[]{:S(2)}) collective-permute-start(bf16[2048,128]{1,0:T(8,128)(2,1)S(1)} %copy-done.4), channel_id=1, source_target_pairs={{0,8},{4,12},{8,0},{12,4},{1,9},{5,13},{9,1},{13,5},{2,10},{6,14},... | collective-permute-start | bytes 1572872 | tf_op jit(solution)/shard_map/ppermute | solution.py:17
  9.4 47.2 %collective-permute-start.4 = (bf16[4096,128]{1,0:T(8,128)(2,1)}, bf16[4096,128]{1,0:T(8,128)(2,1)}, u32[]{:S(2)}, u32[]{:S(2)}) collective-permute-start(bf16[4096,128]{1,0:T(8,128)(2,1)} %get-tuple-element.45.refs_5_), channel_id=1, source_target_pairs={{0,1},{1,0},{2,3},{3,2},{4,5},{5,4},{6,7},{7,6},{8,9},{9,8},{10,11... | collective-permute-start | bytes 3145736 | tf_op jit(solution)/shard_map/ppermute | solution.py:17
  30.6 26.1 %collective-permute-start.5 = (bf16[4096,128]{1,0:T(8,128)(2,1)}, bf16[4096,128]{1,0:T(8,128)(2,1)}, u32[]{:S(2)}, u32[]{:S(2)}) collective-permute-start(bf16[4096,128]{1,0:T(8,128)(2,1)} %collective-permute-done.3.refs_6_), channel_id=1, source_target_pairs={{0,1},{1,0},{2,3},{3,2},{4,5},{5,4},{6,7},{7,6},{8,9},{9,8},{10,11... | collective-permute-start | bytes 3145736 | tf_op jit(solution)/shard_map/ppermute | solution.py:17
  30.6 14.9 %collective-permute-start.1 = (bf16[2048,128]{1,0:T(8,128)(2,1)S(1)}, bf16[2048,128]{1,0:T(8,128)(2,1)S(1)}, u32[]{:S(2)}, u32[]{:S(2)}) collective-permute-start(bf16[2048,128]{1,0:T(8,128)(2,1)S(1)} %copy-done.4), channel_id=1, source_target_pairs={{0,4},{4,0},{8,12},{12,8},{1,5},{5,1},{9,13},{13,9},{2,6},{6,2},{1... | collective-permute-start | bytes 1572872 | tf_op jit(solution)/shard_map/ppermute | solution.py:17
  32.8 23.9 %collective-permute-start.2 = (bf16[2048,128]{1,0:T(8,128)(2,1)}, bf16[2048,128]{1,0:T(8,128)(2,1)}, u32[]{:S(2)}, u32[]{:S(2)}) collective-permute-start(bf16[2048,128]{1,0:T(8,128)(2,1)} %collective-permute-done.refs_2_), channel_id=1, source_target_pairs={{0,4},{4,0},{8,12},{12,8},{1,5},{5,1},{9,13},{13,9},{2,6},{6,2},{1... | collective-permute-start | bytes 1572872 | tf_op jit(solution)/shard_map/ppermute | solution.py:17
  45.5 6.6 %copy-start.5 = (bf16[2048,128]{1,0:T(8,128)(2,1)}, bf16[2048,128]{1,0:T(8,128)(2,1)S(1)}, u32[]{:S(2)}) copy-start(bf16[2048,128]{1,0:T(8,128)(2,1)S(1)} %collective-permute-done.1.refs_3_) | copy-start | bytes 1572868
  45.5 37.1 %collective-permute-start.7 = (bf16[4096,128]{1,0:T(8,128)(2,1)S(1)}, bf16[4096,128]{1,0:T(8,128)(2,1)S(1)}, u32[]{:S(2)}, u32[]{:S(2)}) collective-permute-start(bf16[4096,128]{1,0:T(8,128)(2,1)S(1)} %get-tuple-element.44.refs_5_), channel_id=1, source_target_pairs={{0,1},{1,0},{2,3},{3,2},{4,5},{5,4},{6,7},{7,6},{8,9},{9,8},{10,11... | collective-permute-start | bytes 3145736 | tf_op jit(solution)/shard_map/ppermute | solution.py:17
  52.2 30.5 %copy-start.1 = (bf16[4096,128]{1,0:T(8,128)(2,1)}, bf16[4096,128]{1,0:T(8,128)(2,1)S(1)}, u32[]{:S(2)}) copy-start(bf16[4096,128]{1,0:T(8,128)(2,1)S(1)} %collective-permute-done.6.refs_6_) | copy-start | bytes 3145732
  52.2 30.5 %collective-permute-start.8 = (bf16[4096,128]{1,0:T(8,128)(2,1)S(1)}, bf16[4096,128]{1,0:T(8,128)(2,1)}, u32[]{:S(2)}, u32[]{:S(2)}) collective-permute-start(bf16[4096,128]{1,0:T(8,128)(2,1)S(1)} %collective-permute-done.6.refs_6_), channel_id=1, source_target_pairs={{0,1},{1,0},{2,3},{3,2},{4,5},{5,4},{6,7},{7,6},{8,9},{9,8},{10,11... | collective-permute-start | bytes 3145736 | tf_op jit(solution)/shard_map/ppermute | solution.py:17
  82.6 1.0 copy-start.2
  108.5 4.4 %collective-permute-start.9 = (f32[1,2048]{1,0:T(1,128)}, f32[1,2048]{1,0:T(1,128)S(1)}, u32[]{:S(2)}, u32[]{:S(2)}) collective-permute-start(f32[1,2048]{1,0:T(1,128)} %get-tuple-element.27.refs_11_), channel_id=1, source_target_pairs={{0,4},{4,0},{8,12},{12,8},{1,5},{5,1},{9,13},{13,9},{2,6},{6,2},{1... | collective-permute-start | bytes 24584 | tf_op jit(solution)/shard_map/ppermute | solution.py:17
  110.3 4.8 %collective-permute-start.10 = (f32[1,2048]{1,0:T(1,128)}, f32[1,2048]{1,0:T(1,128)S(1)}, u32[]{:S(2)}, u32[]{:S(2)}) collective-permute-start(f32[1,2048]{1,0:T(1,128)} %get-tuple-element.27.refs_11_), channel_id=1, source_target_pairs={{0,8},{4,12},{8,0},{12,4},{1,9},{5,13},{9,1},{13,5},{2,10},{6,14},... | collective-permute-start | bytes 24584 | tf_op jit(solution)/shard_map/ppermute | solution.py:17
  112.9 5.7 %collective-permute-start.11 = (f32[1,2048]{1,0:T(1,128)}, f32[1,2048]{1,0:T(1,128)S(1)}, u32[]{:S(2)}, u32[]{:S(2)}) collective-permute-start(f32[1,2048]{1,0:T(1,128)} %get-tuple-element.27.refs_11_), channel_id=1, source_target_pairs={{0,12},{4,8},{8,4},{12,0},{1,13},{5,9},{9,5},{13,1},{2,14},{6,10},... | collective-permute-start | bytes 24584 | tf_op jit(solution)/shard_map/ppermute | solution.py:17
  112.9 6.2 %copy-start.12 = (f32[1,2048]{1,0:T(1,128)}, f32[1,2048]{1,0:T(1,128)S(1)}, u32[]{:S(2)}) copy-start(f32[1,2048]{1,0:T(1,128)S(1)} %collective-permute-done.9.refs_12_) | copy-start | bytes 24580
  115.0 4.1 %copy-start.13 = (f32[1,2048]{1,0:T(1,128)}, f32[1,2048]{1,0:T(1,128)S(1)}, u32[]{:S(2)}) copy-start(f32[1,2048]{1,0:T(1,128)S(1)} %collective-permute-done.10.refs_13_) | copy-start | bytes 24580
  118.5 0.6 copy-start.14
  147.3 79.7 %collective-permute-start.20 = (bf16[256,4096]{1,0:T(8,128)(2,1)}, bf16[256,4096]{1,0:T(8,128)(2,1)S(1)}, u32[]{:S(2)}, u32[]{:S(2)}) collective-permute-start(bf16[256,4096]{1,0:T(8,128)(2,1)} %get-tuple-element.43), channel_id=1, source_target_pairs={{0,1},{1,0},{2,3},{3,2},{4,5},{5,4},{6,7},{7,6},{8,9},{9,8},{10,11... | collective-permute-start | bytes 6291464 | tf_op jit(solution)/shard_map/ppermute | solution.py:17
  179.2 14.7 %copy-start.15 = (bf16[1024,256]{1,0:T(8,128)(2,1)S(1)}, bf16[1024,256]{1,0:T(8,128)(2,1)}, u32[]{:S(2)}) copy-start(bf16[1024,256]{1,0:T(8,128)(2,1)} %get-tuple-element.33) | copy-start | bytes 1572868
  193.2 31.5 %copy-start.9 = (f32[1024,256]{1,0:T(8,128)S(1)}, f32[1024,256]{1,0:T(8,128)}, u32[]{:S(2)}) copy-start(f32[1024,256]{1,0:T(8,128)} %get-tuple-element.32) | copy-start | bytes 3145732
  193.2 15.1 %collective-permute-start.14 = (bf16[1024,256]{1,0:T(8,128)(2,1)}, bf16[1024,256]{1,0:T(8,128)(2,1)S(1)}, u32[]{:S(2)}, u32[]{:S(2)}) collective-permute-start(bf16[1024,256]{1,0:T(8,128)(2,1)} %get-tuple-element.37), channel_id=1, source_target_pairs={{0,4},{4,0},{8,12},{12,8},{1,5},{5,1},{9,13},{13,9},{2,6},{6,2},{1... | collective-permute-start | bytes 1572872 | tf_op jit(solution)/shard_map/ppermute | solution.py:17
  193.3 31.6 %collective-permute-start.16 = (bf16[256,2048]{1,0:T(8,128)(2,1)}, bf16[256,2048]{1,0:T(8,128)(2,1)S(1)}, u32[]{:S(2)}, u32[]{:S(2)}) collective-permute-start(bf16[256,2048]{1,0:T(8,128)(2,1)} %get-tuple-element.39), channel_id=1, source_target_pairs={{0,1},{1,0},{2,3},{3,2},{4,5},{5,4},{6,7},{7,6},{8,9},{9,8},{10,11... | collective-permute-start | bytes 3145736 | tf_op jit(solution)/shard_map/ppermute | solution.py:17
  193.9 30.8 %collective-permute-start.12 = (bf16[1024,256]{1,0:T(8,128)(2,1)S(1)}, bf16[1024,256]{1,0:T(8,128)(2,1)S(1)}, u32[]{:S(2)}, u32[]{:S(2)}) collective-permute-start(bf16[1024,256]{1,0:T(8,128)(2,1)S(1)} %copy-done.15), channel_id=1, source_target_pairs={{0,4},{4,0},{8,12},{12,8},{1,5},{5,1},{9,13},{13,9},{2,6},{6,2},{1... | collective-permute-start | bytes 1572872 | tf_op jit(solution)/shard_map/ppermute | solution.py:17
  195.6 34.1 %collective-permute-start.18 = (bf16[256,2048]{1,0:T(8,128)(2,1)}, bf16[256,2048]{1,0:T(8,128)(2,1)S(1)}, u32[]{:S(2)}, u32[]{:S(2)}) collective-permute-start(bf16[256,2048]{1,0:T(8,128)(2,1)} %get-tuple-element.41), channel_id=1, source_target_pairs={{0,1},{1,0},{2,3},{3,2},{4,5},{5,4},{6,7},{7,6},{8,9},{9,8},{10,11... | collective-permute-start | bytes 3145736 | tf_op jit(solution)/shard_map/ppermute | solution.py:17
  209.6 15.3 %copy-start.7 = (f32[256,2048]{1,0:T(8,128)S(1)}, f32[256,2048]{1,0:T(8,128)}, u32[]{:S(2)}) copy-start(f32[256,2048]{1,0:T(8,128)} %get-tuple-element.38) | copy-start | bytes 6291460
  209.7 22.6 %collective-permute-start.15 = (bf16[1024,128]{1,0:T(8,128)(2,1)S(1)}, bf16[1024,128]{1,0:T(8,128)(2,1)S(1)}, u32[]{:S(2)}, u32[]{:S(2)}) collective-permute-start(bf16[1024,128]{1,0:T(8,128)(2,1)S(1)} %slice.73), channel_id=1, source_target_pairs={{0,8},{4,12},{8,0},{12,4},{1,9},{5,13},{9,1},{13,5},{2,10},{6,14},... | collective-permute-start | bytes 786440 | tf_op jit(solution)/shard_map/ppermute | solution.py:17
  224.9 13.3 %collective-permute-start.13 = (bf16[1024,128]{1,0:T(8,128)(2,1)S(1)}, bf16[1024,128]{1,0:T(8,128)(2,1)S(1)}, u32[]{:S(2)}, u32[]{:S(2)}) collective-permute-start(bf16[1024,128]{1,0:T(8,128)(2,1)S(1)} %slice.74), channel_id=1, source_target_pairs={{0,8},{4,12},{8,0},{12,4},{1,9},{5,13},{9,1},{13,5},{2,10},{6,14},... | collective-permute-start | bytes 786440 | tf_op jit(solution)/shard_map/ppermute | solution.py:17
  225.0 2.2 copy-start.3
  225.4 50.4 %collective-permute-start.17 = (bf16[128,2048]{1,0:T(8,128)(2,1)S(1)}, bf16[128,2048]{1,0:T(8,128)(2,1)S(1)}, u32[]{:S(2)}, u32[]{:S(2)}) collective-permute-start(bf16[128,2048]{1,0:T(8,128)(2,1)S(1)} %slice.72), channel_id=1, source_target_pairs={{0,2},{1,3},{2,0},{3,1},{4,6},{5,7},{6,4},{7,5},{8,10},{9,11},{10,... | collective-permute-start | bytes 1572872 | tf_op jit(solution)/shard_map/ppermute | solution.py:17
  227.9 1.7 copy-start.6
  228.1 34.6 %collective-permute-start.21 = (bf16[128,4096]{1,0:T(8,128)(2,1)S(1)}, bf16[128,4096]{1,0:T(8,128)(2,1)S(1)}, u32[]{:S(2)}, u32[]{:S(2)}) collective-permute-start(bf16[128,4096]{1,0:T(8,128)(2,1)S(1)} %slice.70), channel_id=1, source_target_pairs={{0,2},{1,3},{2,0},{3,1},{4,6},{5,7},{6,4},{7,5},{8,10},{9,11},{10,... | collective-permute-start | bytes 3145736 | tf_op jit(solution)/shard_map/ppermute | solution.py:17
  230.9 41.7 %collective-permute-start.19 = (bf16[128,2048]{1,0:T(8,128)(2,1)}, bf16[128,2048]{1,0:T(8,128)(2,1)S(1)}, u32[]{:S(2)}, u32[]{:S(2)}) collective-permute-start(bf16[128,2048]{1,0:T(8,128)(2,1)} %slice.71), channel_id=1, source_target_pairs={{0,2},{1,3},{2,0},{3,1},{4,6},{5,7},{6,4},{7,5},{8,10},{9,11},{10,... | collective-permute-start | bytes 1572872 | tf_op jit(solution)/shard_map/ppermute | solution.py:17
  262.7 1.0 copy-start.8
  272.6 0.8 copy-start.11
  275.8 0.8 copy-start.10
